TPU v7x, 32 devices: a whole 2x2x4 slice. The times are simulated.
32 devices in a mesh: dp: 8 (over y, x, core), mp: 4 (over z).
Axes of the slice: x: 2, y: 2, z: 4, core: 2. Of those that a mesh axis runs over, the one named last changes fastest.
Arguments:
- patches: bfloat16 [1024, 6144], P('dp', 'mp'), may hold values from -64 to 64
- send_start: int32 [8, 8], P('dp'), may hold values from 0 to 128, as said below
- run_length: int32 [8, 8], P('dp'), may hold values from 0 to 32, as said below
- slot_start: int32 [8, 8], P('dp'), may hold values from 0 to 128, as said below
- image_ids: int32 [8, 128], P('dp'), may hold values from 0 to 7, never falling along the last dimension, each value on 1 to 32 neighbouring positions
- norm_gain: float32 [6144], replicated, may hold values from 0.1 to 1.9
- qkv_weight: bfloat16 [6144, 3, 4096], P('dp', None, 'mp'), may hold values from -0.078125 to 0.078125
- query_gain: float32 [128], replicated, may hold values from 0.1 to 1.9
- key_gain: float32 [128], replicated, may hold values from 0.1 to 1.9
- out_weight: bfloat16 [4096, 6144], P('mp'), may hold values from -0.09375 to 0.09375
Outputs:
- packed: bfloat16 [1024, 6144], P('dp', 'mp')
- attended: bfloat16 [1024, 6144], P('dp', 'mp')
Inputs may be any that keep to these rules, and one draw needn't show every extreme that they name: `run_length`: every source's runs sum to 128 and every pack's runs sum to 128; the longest run is exactly 32. `send_start`: the runs of one source device do not intersect and cover its 128 rows. `slot_start`: the runs into one pack do not intersect and fill its 128 slots. `image_ids`: image numbers never fall along a pack; equal numbers mark one image.
All inputs are finite; a program needn't handle non-finite values.
Results may differ from a plain program's by a relative error of at most 0.011.
Values may be sent and summed in bfloat16 or wider, within the bound.
A program may use at most 128 MiB of HBM per device.

v0:
```python
import jax
import jax.numpy as jnp
from jax import lax
from jax.sharding import PartitionSpec as P

epsilon = 1e-06


def row_norm(values, scales):
    middle = jnp.mean(values, axis=-1, keepdims=True)
    spread = jnp.mean(values * values, axis=-1, keepdims=True) - middle * middle
    return (values - middle) * lax.rsqrt(spread + epsilon) * scales


def on_device(
    patches,
    send_start,
    run_length,
    slot_start,
    image_ids,
    norm_gain,
    qkv_weight,
    query_gain,
    key_gain,
    out_weight,
):
    pack_rows, feat_local = patches.shape
    pack_count = lax.axis_size("dp")
    mp_count = lax.axis_size("mp")
    capacity = 2 * pack_rows // pack_count
    local_cols = qkv_weight.shape[1] * qkv_weight.shape[2]
    offsets = jnp.arange(capacity, dtype=jnp.int32)
    rows = jnp.arange(pack_rows, dtype=jnp.int32)
    x = patches.astype(jnp.float32)
    sums = jnp.stack([jnp.sum(x, axis=-1), jnp.sum(x * x, axis=-1)])
    sums = lax.psum(sums, "mp") / (feat_local * mp_count)
    middle = sums[0][:, None]
    spread = sums[1][:, None] - middle * middle
    gain = lax.dynamic_slice_in_dim(norm_gain, lax.axis_index("mp") * feat_local, feat_local)
    normed = ((x - middle) * lax.rsqrt(spread + epsilon) * gain).astype(jnp.bfloat16)
    wide = lax.all_gather(normed, "mp", axis=1, tiled=True)
    slices = lax.all_to_all(wide, "dp", split_axis=1, concat_axis=0, tiled=True)
    tables = jnp.concatenate([send_start, run_length, slot_start], axis=0)[None]
    tables = lax.all_gather(tables, "dp", axis=0, tiled=True)
    starts, lengths, slots = (tables[:, 0].T, tables[:, 1].T, tables[:, 2])
    inside = (rows >= slots[:, :, None]) & (rows < (slots + lengths)[:, :, None])
    base = jnp.arange(pack_count, dtype=jnp.int32)[None, :] * pack_rows + starts - slots
    origin = jnp.sum(jnp.where(inside, base[:, :, None] + rows, 0), axis=1).reshape(-1)
    chosen = (origin[:, None] == jnp.arange(origin.shape[0], dtype=jnp.int32)).astype(jnp.bfloat16)
    ordered = jnp.dot(chosen, slices, preferred_element_type=jnp.float32).astype(jnp.bfloat16)
    partial = jnp.dot(
        ordered,
        qkv_weight.reshape(qkv_weight.shape[0], local_cols),
        preferred_element_type=jnp.float32,
    ).astype(jnp.bfloat16)
    projected = lax.psum_scatter(partial, "dp", scatter_dimension=0, tiled=True).astype(jnp.float32)
    own_rows = send_start[0][:, None] + offsets[None, :]
    occupied = offsets[None, :] < run_length[0][:, None]
    pick = (occupied[:, :, None] & (own_rows[:, :, None] == rows)).astype(jnp.bfloat16)
    outgoing = jnp.dot(
        pick.reshape(-1, pack_rows), patches, preferred_element_type=jnp.float32
    ).astype(jnp.bfloat16)
    arrived = lax.all_to_all(
        outgoing.reshape(pack_count, capacity, feat_local),
        "dp",
        split_axis=0,
        concat_axis=0,
        tiled=True,
    )
    targets = (slot_start[0][:, None] + offsets[None, :]).reshape(-1)
    place = (rows[:, None] == targets[None, :]).astype(jnp.bfloat16)
    packed = jnp.dot(
        place, arrived.reshape(-1, feat_local), preferred_element_type=jnp.float32
    ).astype(jnp.bfloat16)
    head_size = query_gain.shape[0]
    heads_here = qkv_weight.shape[2] // head_size
    split_heads = projected.reshape(pack_rows, 3, heads_here, head_size)
    queries = row_norm(split_heads[:, 0], query_gain).astype(jnp.bfloat16)
    key_rows = row_norm(split_heads[:, 1], key_gain).astype(jnp.bfloat16)
    values = split_heads[:, 2].astype(jnp.bfloat16)
    scores = jnp.einsum(
        "qhd,khd->hqk", queries, key_rows, preferred_element_type=jnp.float32
    ) * head_size ** (-0.5)
    image_of = image_ids[0]
    same_image = image_of[:, None] == image_of[None, :]
    weights_raw = jnp.where(same_image[None], jnp.exp(scores), 0.0)
    totals = jnp.sum(weights_raw, axis=-1, keepdims=True)
    attention = (weights_raw / totals).astype(jnp.bfloat16)
    context = jnp.einsum(
        "hqk,khd->qhd", attention, values, preferred_element_type=jnp.float32
    ).astype(jnp.bfloat16)
    context = context.reshape(pack_rows, heads_here * head_size)
    partial_value = jnp.dot(context, out_weight, preferred_element_type=jnp.float32)
    attended = lax.psum_scatter(
        partial_value.astype(jnp.bfloat16), "mp", scatter_dimension=1, tiled=True
    )
    return (packed, attended)


def solution(mesh):
    return jax.shard_map(
        on_device,
        mesh=mesh,
        in_specs=(
            P("dp", "mp"),
            P("dp", None),
            P("dp", None),
            P("dp", None),
            P("dp", None),
            P(),
            P("dp", None, "mp"),
            P(),
            P(),
            P("mp", None),
        ),
        out_specs=(P("dp", "mp"), P("dp", "mp")),
        check_vma=False,
    )
```

profile of v0, /device:TPU:0, one launch (start us, length us, event | category | flops | bytes accessed | tf_op | source)
XLA Modules:
  0.0 220.3 jit_solution(4133471638652877734)
XLA Ops:
  7.2 1.2 copy.47
  8.4 0.2 convert_reduce_fusion
  8.7 13.5 %psum.7 = f32[2,128]{1,0:T(2,128)S(1)} all-reduce(f32[2,128]{1,0:T(2,128)S(1)} %pad_maximum_fusion), channel_id=1, replica_groups=mesh['dp'=8,'mp'=4] {'mp'}, use_global_device_ids=true, to_apply=%region_3.4 | all-reduce | flops 256 | bytes 2048 | tf_op jit(solution)/shard_map/psum | solution.py:36
  22.1 0.8 dynamic_slice.3
  22.9 1.0 fusion.8
  24.0 35.5 %all-gather.4.cloned.1.call-done = bf16[128,6144]{0,1:T(8,128)(2,1)} async-done(((bf16[128,1536]{0,1:T(8,128)(2,1)}), bf16[128,6144]{0,1:T(8,128)(2,1)}) %all-gather.4.cloned.1.call-update) | async-done | bytes 1572880 | tf_op jit(solution)/shard_map/all_gather | solution.py:41
  59.4 3.8 %all-to-all-start.1 = ((bf16[128,8,768]{0,2,1:T(8,128)(2,1)}), bf16[128,8,768]{0,2,1:T(8,128)(2,1)S(1)}, u32[]{:S(2)}, u32[]{:S(2)}) async-start(bf16[128,8,768]{0,2,1:T(8,128)(2,1)} %bitcast.83), calls=%async_computation.1 | async-start | bytes 3145728 | tf_op jit(solution)/shard_map/all_to_all | solution.py:42
  63.3 24.0 %all-gather.1 = s32[8,3,8]{2,1,0:T(4,128)S(1)} all-gather(s32[1,3,8]{2,1,0:T(4,128)S(1)} %add_bitcast_fusion), channel_id=2, replica_groups=mesh['dp'=8,'mp'=4] {'dp'}, dimensions={0}, use_global_device_ids=true | all-gather | bytes 864 | tf_op jit(solution)/shard_map/all_gather | solution.py:44
  87.5 6.7 %copy.49 = bf16[768,3,1024]{0,2,1:T(8,128)(2,1)} copy(bf16[768,3,1024]{2,0,1:T(8,128)(2,1)} %param.16) | data formatting | bytes 9437184 | tf_op args[6]
  94.2 0.1 select_reduce_fusion
  94.3 0.7 copy.48
  95.0 12.2 %convolution_convert_fusion.1 = bf16[1024,3072]{1,0:T(8,128)(2,1)} fusion(bf16[768,3072]{0,1:T(8,128)(2,1)} %bitcast.79, bf16[1024,768]{1,0:T(8,128)(2,1)S(1)} %bitcast.84, s32[1024]{0:T(1024)S(1)} %bitcast.91), kind=kOutput, calls=%fused_computation.1 | convolution fusion | flops 6447431680 | bytes 12587008 | tf_op jit(solution)/shard_map/dot_general | solution.py:51
  107.4 0.6 copy-done.1
  107.9 0.1 broadcast_compare_fusion
  108.0 59.1 %reduce-scatter.3.cloned.1.call-done = bf16[128,3072]{1,0:T(8,128)(2,1)} async-done(((bf16[1024,3072]{1,0:T(8,128)(2,1)}), bf16[128,3072]{1,0:T(8,128)(2,1)}) %reduce-scatter.3.cloned.1.call-update) | async-done | bytes 786448 | tf_op jit(solution)/shard_map/reduce_scatter | solution.py:56
  167.2 1.3 copy.58
  168.5 0.2 copy_convert_fusion
  168.7 0.3 slice_reduce_fusion.1
  169.0 0.3 fusion.16
  169.4 0.2 copy.57
  169.7 0.7 fusion.4
  170.4 0.3 convolution_convert_fusion.4
  170.7 7.6 %convolution_convert_fusion = bf16[128,6144]{1,0:T(8,128)(2,1)} fusion(bf16[128,1024]{0,1:T(8,128)(2,1)S(1)} %bitcast.86, bf16[1024,6144]{1,0:T(8,128)(2,1)} %param.19), kind=kOutput, calls=%fused_computation | convolution fusion | flops 1611399168 | bytes 14417920 | tf_op jit(solution)/shard_map/dot_general | solution.py:93
  178.4 0.1 add.117
  178.5 0.1 lt.37
  178.6 0.7 copy-done
  179.3 1.3 convolution_convert_fusion.2
  180.6 3.5 %all-to-all-start = ((bf16[8,32,1536]{2,1,0:T(8,128)(2,1)}), bf16[8,32,1536]{2,1,0:T(8,128)(2,1)S(1)}, u32[]{:S(2)}, u32[]{:S(2)}) async-start(bf16[8,32,1536]{2,1,0:T(8,128)(2,1)} %bitcast.3), calls=%async_computation | async-start | bytes 1572864 | tf_op jit(solution)/shard_map/all_to_all | solution.py:63
  184.2 0.1 add.111
  184.3 12.4 %all-to-all-done = bf16[8,32,1536]{2,1,0:T(8,128)(2,1)S(1)} async-done(((bf16[8,32,1536]{2,1,0:T(8,128)(2,1)}), bf16[8,32,1536]{2,1,0:T(8,128)(2,1)S(1)}, u32[]{:S(2)}, u32[]{:S(2)}) %all-to-all-start) | async-done | bytes 786464 | tf_op jit(solution)/shard_map/all_to_all | solution.py:63
  196.7 1.0 convolution_convert_fusion.3
  197.7 16.0 %reduce-scatter.5.cloned.1.call-done = bf16[128,1536]{1,0:T(8,128)(2,1)} async-done(((bf16[128,6144]{1,0:T(8,128)(2,1)}), bf16[128,1536]{1,0:T(8,128)(2,1)}) %reduce-scatter.5.cloned.1.call-update) | async-done | bytes 393232 | tf_op jit(solution)/shard_map/reduce_scatter | solution.py:94
  (34 shorter events, 0.6 us)
Async XLA Ops:
  7.2 52.3 %all-gather.4.cloned.1.call-start = ((), (), s32[]{:S(2)}) async-start(), calls=%async_computation.4 | async-start | bytes 1966080 | tf_op jit(solution)/shard_map/all_gather | solution.py:41
  59.4 3.8 %copy-start.2 = (s32[1,8]{1,0:T(1,128)S(1)}, s32[1,8]{1,0:T(1,128)}, u32[]{:S(2)}) copy-start(s32[1,8]{1,0:T(1,128)} %param.11) | copy-start | bytes 100
  59.4 3.8 %copy-start.3 = (s32[1,8]{1,0:T(1,128)S(1)}, s32[1,8]{1,0:T(1,128)}, u32[]{:S(2)}) copy-start(s32[1,8]{1,0:T(1,128)} %param.13) | copy-start | bytes 100
  59.4 3.9 %copy-start.4 = (s32[1,8]{1,0:T(1,128)S(1)}, s32[1,8]{1,0:T(1,128)}, u32[]{:S(2)}) copy-start(s32[1,8]{1,0:T(1,128)} %param.12) | copy-start | bytes 100
  59.4 34.9 %all-to-all-start.1 = ((bf16[128,8,768]{0,2,1:T(8,128)(2,1)}), bf16[128,8,768]{0,2,1:T(8,128)(2,1)S(1)}, u32[]{:S(2)}, u32[]{:S(2)}) async-start(bf16[128,8,768]{0,2,1:T(8,128)(2,1)} %bitcast.83), calls=%async_computation.1 | async-start | bytes 3145728 | tf_op jit(solution)/shard_map/all_to_all | solution.py:42
  63.2 103.9 %reduce-scatter.3.cloned.1.call-start = ((), (), s32[]{:S(2)}) async-start(), calls=%async_computation.5 | async-start | bytes 7077888 | tf_op jit(solution)/shard_map/reduce_scatter | solution.py:56
  107.3 0.7 copy-start.1
  107.3 106.4 %reduce-scatter.5.cloned.1.call-start = ((), (), s32[]{:S(2)}) async-start(), calls=%async_computation.6 | async-start | bytes 1966080 | tf_op jit(solution)/shard_map/reduce_scatter | solution.py:94
  168.6 1.0 copy-start.5
  168.7 1.0 copy-start.6
  178.3 1.0 copy-start
  180.6 16.1 %all-to-all-start = ((bf16[8,32,1536]{2,1,0:T(8,128)(2,1)}), bf16[8,32,1536]{2,1,0:T(8,128)(2,1)S(1)}, u32[]{:S(2)}, u32[]{:S(2)}) async-start(bf16[8,32,1536]{2,1,0:T(8,128)(2,1)} %bitcast.3), calls=%async_computation | async-start | bytes 1572864 | tf_op jit(solution)/shard_map/all_to_all | solution.py:63
Sparse Core Ops, SparseCore 0:
  24.1 35.2 all-gather.3
  107.4 59.6 reduce-scatter.2
  178.4 35.2 reduce-scatter.4
where the time goes:
time: 221 us; the launch traced here: 220 us
  waiting for transfers between devices  123 us (56%)
  blocking collectives  37.5 us (17%)
  matrix products  23.2 us (10%)
  between operations  13.9 us (6%)
  local copies, waits for them, and re-layouts  12.6 us (6%)
  starting transfers between devices  7.45 us (3%)
  other arithmetic  2.56 us (1%)
    reduce_scatter x1, waiting for transfers between devices, on_device(): lax.psum_scatter(partial, 'dp', scatter_dimension=0, tiled=True)  59.1 us
    all_gather x1, waiting for transfers between devices, on_device(): wide = lax.all_gather(normed, 'mp', axis=1, tiled=True)  35.5 us
    all_gather x1, blocking collectives, on_device(): tables = lax.all_gather(tables, 'dp', axis=0, tiled=True)  24 us
    reduce_scatter x1, waiting for transfers between devices, on_device(): lax.psum_scatter(partial_value.astype(jnp.bfloat16), 'mp', scatter_dimens...  16 us
    psum x1, blocking collectives, on_device(): sums = lax.psum(sums, 'mp') / (feat_local * mp_count)  13.5 us
    all_to_all x1, waiting for transfers between devices, on_device(): lax.all_to_all(outgoing.reshape(pack_count, capacity, feat_local), 'dp',...  12.4 us
    dot_general x1, matrix products, on_device(): jnp.dot(ordered, qkv_weight.reshape(qkv_weight.shape[0], local_cols), pre...  12.2 us
    unnamed x18, local copies, waits for them, and re-layouts  10.7 us
  transfers between devices with their start and end apart: 5, of which 4 were waited for; matrix products, arithmetic and copies ran while one was open for 4% of the time, Pallas kernels for 0%

commit v1 on v0

--- a/solution.py
+++ b/solution.py
@@ -39,7 +39,10 @@
     gain = lax.dynamic_slice_in_dim(norm_gain, lax.axis_index("mp") * feat_local, feat_local)
     normed = ((x - middle) * lax.rsqrt(spread + epsilon) * gain).astype(jnp.bfloat16)
     wide = lax.all_gather(normed, "mp", axis=1, tiled=True)
-    slices = lax.all_to_all(wide, "dp", split_axis=1, concat_axis=0, tiled=True)
+    size = lax.axis_size("dp")
+    blocks = jnp.stack(jnp.split(wide, size, axis=1), axis=0)
+    blocks = lax.all_to_all(blocks, "dp", split_axis=0, concat_axis=0)
+    slices = jnp.concatenate(blocks, axis=0)
     tables = jnp.concatenate([send_start, run_length, slot_start], axis=0)[None]
     tables = lax.all_gather(tables, "dp", axis=0, tiled=True)
     starts, lengths, slots = (tables[:, 0].T, tables[:, 1].T, tables[:, 2])

time: 221 us -> 234 us (1.059)
  local copies, waits for them, and re-layouts: 12.6 us -> 23.6 us
    unnamed x18 -> x24, local copies, waits for them, and re-layouts: 10.7 us -> 20.7 us
where the time goes in v1:
time: 234 us; the launch traced here: 233 us
  waiting for transfers between devices  123 us (53%)
  blocking collectives  37.5 us (16%)
  local copies, waits for them, and re-layouts  23.6 us (10%)
  matrix products  23.2 us (10%)
  between operations  13.9 us (6%)
  starting transfers between devices  7.45 us (3%)
  other arithmetic  4.52 us (2%)
    reduce_scatter x1, waiting for transfers between devices, on_device(): lax.psum_scatter(partial, 'dp', scatter_dimension=0, tiled=True)  59.1 us
    all_gather x1, waiting for transfers between devices, on_device(): wide = lax.all_gather(normed, 'mp', axis=1, tiled=True)  35.5 us
    all_gather x1, blocking collectives, on_device(): tables = lax.all_gather(tables, 'dp', axis=0, tiled=True)  24 us
    unnamed x24, local copies, waits for them, and re-layouts  20.7 us
    reduce_scatter x1, waiting for transfers between devices, on_device(): lax.psum_scatter(partial_value.astype(jnp.bfloat16), 'mp', scatter_dimens...  16 us
    psum x1, blocking collectives, on_device(): sums = lax.psum(sums, 'mp') / (feat_local * mp_count)  13.5 us
    all_to_all x1, waiting for transfers between devices, on_device(): lax.all_to_all(outgoing.reshape(pack_count, capacity, feat_local), 'dp',...  12.4 us
    dot_general x1, matrix products, on_device(): jnp.dot(ordered, qkv_weight.reshape(qkv_weight.shape[0], local_cols), pre...  12.2 us
  transfers between devices with their start and end apart: 5, of which 4 were waited for; matrix products, arithmetic and copies ran while one was open for 4% of the time, Pallas kernels for 0%

profile of v1, /device:TPU:0, one launch (start us, length us, event | category | flops | bytes accessed | tf_op | source)
XLA Modules:
  0.0 233.2 jit_solution(4764018125740296791)
XLA Ops:
  7.2 1.2 convert_reduce_fusion
  8.4 13.5 %psum.7 = f32[2,128]{1,0:T(2,128)S(1)} all-reduce(f32[2,128]{1,0:T(2,128)S(1)} %pad_maximum_fusion), channel_id=1, replica_groups=mesh['dp'=8,'mp'=4] {'mp'}, use_global_device_ids=true, to_apply=%region_3.4 | all-reduce | flops 256 | bytes 2048 | tf_op jit(solution)/shard_map/psum | solution.py:36
  21.9 0.8 dynamic_slice.3
  22.7 2.0 fusion.8
  24.7 35.5 %all-gather.4.cloned.1.call-done = bf16[128,6144]{1,0:T(8,128)(2,1)} async-done(((bf16[128,1536]{1,0:T(8,128)(2,1)}), bf16[128,6144]{1,0:T(8,128)(2,1)}) %all-gather.4.cloned.1.call-update) | async-done | bytes 1572880 | tf_op jit(solution)/shard_map/all_gather | solution.py:41
  60.2 1.6 fusion.35
  61.8 1.6 fusion.34
  63.4 1.6 fusion.33
  65.0 1.6 fusion.32
  66.6 1.6 fusion.31
  68.2 1.6 fusion.30
  69.8 1.6 fusion.29
  71.5 1.6 fusion.28
  73.1 3.8 %all-to-all-start.1 = ((bf16[8,128,768]{2,1,0:T(8,128)(2,1)}), bf16[8,128,768]{2,1,0:T(8,128)(2,1)S(1)}, u32[]{:S(2)}, u32[]{:S(2)}) async-start(bf16[8,128,768]{2,1,0:T(8,128)(2,1)} %fusion.28), calls=%async_computation.1 | async-start | bytes 3145728 | tf_op jit(solution)/shard_map/all_to_all | solution.py:44
  77.0 24.0 %all-gather.1 = s32[8,3,8]{2,1,0:T(4,128)S(1)} all-gather(s32[1,3,8]{2,1,0:T(4,128)S(1)} %add_bitcast_fusion), channel_id=2, replica_groups=mesh['dp'=8,'mp'=4] {'dp'}, dimensions={0}, use_global_device_ids=true | all-gather | bytes 864 | tf_op jit(solution)/shard_map/all_gather | solution.py:47
  101.1 6.7 %copy.37 = bf16[768,3,1024]{0,2,1:T(8,128)(2,1)} copy(bf16[768,3,1024]{2,0,1:T(8,128)(2,1)} %param.16) | data formatting | bytes 9437184 | tf_op args[6]
  108.0 12.2 %convolution_convert_fusion.1 = bf16[1024,3072]{1,0:T(8,128)(2,1)} fusion(bf16[768,3072]{0,1:T(8,128)(2,1)} %bitcast.108, bf16[1024,768]{1,0:T(8,128)(2,1)S(1)} %bitcast.112, s32[1024]{0:T(1024)S(1)} %bitcast.119), kind=kOutput, calls=%fused_computation.1 | convolution fusion | flops 6447431680 | bytes 12587008 | tf_op jit(solution)/shard_map/dot_general | solution.py:54
  120.3 0.6 copy-done.1
  121.0 59.1 %reduce-scatter.3.cloned.1.call-done = bf16[128,3072]{1,0:T(8,128)(2,1)} async-done(((bf16[1024,3072]{1,0:T(8,128)(2,1)}), bf16[128,3072]{1,0:T(8,128)(2,1)}) %reduce-scatter.3.cloned.1.call-update) | async-done | bytes 786448 | tf_op jit(solution)/shard_map/reduce_scatter | solution.py:59
  180.1 1.3 copy.46
  181.6 0.3 slice_reduce_fusion.1
  181.9 0.3 fusion.16
  182.3 0.2 copy.45
  182.6 0.7 fusion.4
  183.3 0.3 convolution_convert_fusion.4
  183.6 7.6 %convolution_convert_fusion = bf16[128,6144]{1,0:T(8,128)(2,1)} fusion(bf16[128,1024]{0,1:T(8,128)(2,1)S(1)} %bitcast.114, bf16[1024,6144]{1,0:T(8,128)(2,1)} %param.19), kind=kOutput, calls=%fused_computation | convolution fusion | flops 1611399168 | bytes 14417920 | tf_op jit(solution)/shard_map/dot_general | solution.py:96
  191.6 0.7 copy-done
  192.2 1.3 convolution_convert_fusion.2
  193.5 3.5 %all-to-all-start = ((bf16[8,32,1536]{2,1,0:T(8,128)(2,1)}), bf16[8,32,1536]{2,1,0:T(8,128)(2,1)S(1)}, u32[]{:S(2)}, u32[]{:S(2)}) async-start(bf16[8,32,1536]{2,1,0:T(8,128)(2,1)} %bitcast.3), calls=%async_computation | async-start | bytes 1572864 | tf_op jit(solution)/shard_map/all_to_all | solution.py:66
  197.2 12.4 %all-to-all-done = bf16[8,32,1536]{2,1,0:T(8,128)(2,1)S(1)} async-done(((bf16[8,32,1536]{2,1,0:T(8,128)(2,1)}), bf16[8,32,1536]{2,1,0:T(8,128)(2,1)S(1)}, u32[]{:S(2)}, u32[]{:S(2)}) %all-to-all-start) | async-done | bytes 786464 | tf_op jit(solution)/shard_map/all_to_all | solution.py:66
  209.6 1.0 convolution_convert_fusion.3
  210.6 16.0 %reduce-scatter.5.cloned.1.call-done = bf16[128,1536]{1,0:T(8,128)(2,1)} async-done(((bf16[128,6144]{1,0:T(8,128)(2,1)}), bf16[128,1536]{1,0:T(8,128)(2,1)}) %reduce-scatter.5.cloned.1.call-update) | async-done | bytes 393232 | tf_op jit(solution)/shard_map/reduce_scatter | solution.py:97
  (40 shorter events, 1.2 us)
Async XLA Ops:
  7.2 53.0 %all-gather.4.cloned.1.call-start = ((), (), s32[]{:S(2)}) async-start(), calls=%async_computation.4 | async-start | bytes 1966080 | tf_op jit(solution)/shard_map/all_gather | solution.py:41
  73.1 3.8 %copy-start.2 = (s32[1,8]{1,0:T(1,128)S(1)}, s32[1,8]{1,0:T(1,128)}, u32[]{:S(2)}) copy-start(s32[1,8]{1,0:T(1,128)} %param.11) | copy-start | bytes 100
  73.1 3.8 %copy-start.3 = (s32[1,8]{1,0:T(1,128)S(1)}, s32[1,8]{1,0:T(1,128)}, u32[]{:S(2)}) copy-start(s32[1,8]{1,0:T(1,128)} %param.13) | copy-start | bytes 100
  73.1 3.9 %copy-start.4 = (s32[1,8]{1,0:T(1,128)S(1)}, s32[1,8]{1,0:T(1,128)}, u32[]{:S(2)}) copy-start(s32[1,8]{1,0:T(1,128)} %param.12) | copy-start | bytes 100
  73.1 34.9 %all-to-all-start.1 = ((bf16[8,128,768]{2,1,0:T(8,128)(2,1)}), bf16[8,128,768]{2,1,0:T(8,128)(2,1)S(1)}, u32[]{:S(2)}, u32[]{:S(2)}) async-start(bf16[8,128,768]{2,1,0:T(8,128)(2,1)} %fusion.28), calls=%async_computation.1 | async-start | bytes 3145728 | tf_op jit(solution)/shard_map/all_to_all | solution.py:44
  76.9 103.2 %reduce-scatter.3.cloned.1.call-start = ((), (), s32[]{:S(2)}) async-start(), calls=%async_computation.5 | async-start | bytes 7077888 | tf_op jit(solution)/shard_map/reduce_scatter | solution.py:59
  120.2 0.7 copy-start.1
  120.2 106.4 %reduce-scatter.5.cloned.1.call-start = ((), (), s32[]{:S(2)}) async-start(), calls=%async_computation.6 | async-start | bytes 1966080 | tf_op jit(solution)/shard_map/reduce_scatter | solution.py:97
  181.6 1.0 copy-start.5
  181.6 1.0 copy-start.6
  191.2 1.0 copy-start
  193.5 16.1 %all-to-all-start = ((bf16[8,32,1536]{2,1,0:T(8,128)(2,1)}), bf16[8,32,1536]{2,1,0:T(8,128)(2,1)S(1)}, u32[]{:S(2)}, u32[]{:S(2)}) async-start(bf16[8,32,1536]{2,1,0:T(8,128)(2,1)} %bitcast.3), calls=%async_computation | async-start | bytes 1572864 | tf_op jit(solution)/shard_map/all_to_all | solution.py:66
Sparse Core Ops, SparseCore 0:
  24.8 35.2 all-gather.3
  120.4 59.6 reduce-scatter.2
  191.4 35.2 reduce-scatter.4
